TPU v7x, 768 devices: a whole 4x8x12 slice. The times are simulated.
768 devices in a mesh: section: 192 (over y, z_lo, x, core), expert: 4 (over z_hi).
Axes of the slice: x: 4, y: 8, z: 12 (z_hi: 4, z_lo: 3; z = z_hi * 3 + z_lo), core: 2. Of those that a mesh axis runs over, the one named last changes fastest.
Arguments:
- routes: int32 [192, 2, 256, 2], P('section'), may hold values from 0 to 3, all different within a row; in each aligned block of 256 rows (0 to 255, 256 to 511, ..., all dimensions but the last counted through in order) at most 192 rows name the same one
- x_blocks: bfloat16 [192, 2, 4, 192, 1024], P('section', None, 'expert'), may hold values from -6 to 6
- d_hidden: bfloat16 [192, 2, 4, 192, 384], P('section', None, 'expert'), may hold values from -3 to 3
- weights: bfloat16 [192, 4, 1024, 768], P('section', 'expert'), as said below
Outputs:
- d_in: bfloat16 [192, 256, 2, 1024], P('section', 'expert')
- d_weights: bfloat16 [192, 4, 1024, 768], P('section', 'expert')
Inputs may be any that keep to these rules, and one draw needn't show every extreme that they name: weights[s] equals weights[(s + 96) mod 192] for every section s: twin sections hold copies of one layer. `routes`: each token names 2 different experts; in each section and direction no expert is named by more than 192 tokens, and in every draw some expert is named by exactly 192 tokens of some section and direction.
All inputs are finite; a program needn't handle non-finite values.
Results may differ from a plain program's by a relative error of at most 0.0059.
Values may be sent and summed in bfloat16 or wider, within the bound.
A program may use at most 32 MiB of HBM per device.

v0:
```python
import jax
import jax.numpy as jnp
from jax import lax
from jax.sharding import PartitionSpec as P


def from_behind(block, axis, distance):
    devices = range(lax.axis_size(axis))
    route = [(i - distance, i) for i in devices if i - distance in devices]
    return lax.ppermute(block, axis, route)


def passed_along(block, axis, distance):
    devices = range(lax.axis_size(axis))
    route = [((i - distance) % len(devices), i) for i in devices]
    return lax.ppermute(block, axis, route)


def expert_backward(flat_in, flat_grad, matrix):
    hidden_width = flat_grad.shape[1]
    projected = jnp.dot(flat_in, matrix, preferred_element_type=jnp.float32)
    gate_pre = projected[:, :hidden_width]
    up_pre = projected[:, hidden_width:]
    sigmoid = jax.nn.sigmoid(gate_pre)
    grad_float = flat_grad.astype(jnp.float32)
    grad_gate = grad_float * up_pre * sigmoid * (1.0 + gate_pre * (1.0 - sigmoid))
    grad_up = grad_float * gate_pre * sigmoid
    return jnp.concatenate([grad_gate, grad_up], axis=1).astype(jnp.bfloat16)


def weight_product(flat_in, grad_pre):
    return lax.dot_general(
        flat_in, grad_pre, (((0,), (0,)), ((), ())), preferred_element_type=jnp.float32
    ).astype(jnp.bfloat16)


def body(routes, x_blocks, d_hidden, weights):
    expert_index = lax.axis_index("expert")
    routing = routes[0]
    capacity = x_blocks.shape[3]
    width = x_blocks.shape[4]
    hidden_width = d_hidden.shape[4]
    routed = jnp.any(routing == expert_index, axis=-1)
    slot_index = jnp.cumsum(routed.astype(jnp.int32), axis=1) - 1
    live_count = jnp.sum(routed.astype(jnp.int32), axis=1)
    live_slot = lax.broadcasted_iota(jnp.int32, (2, capacity), 1) < live_count[:, None]
    inputs = x_blocks[0, :, 0]
    grads = jnp.where(live_slot[..., None], d_hidden[0, :, 0], jnp.zeros((), jnp.bfloat16))
    matrix = weights[0, 0]
    flat_in = inputs.reshape(2 * capacity, width)
    flat_grad = grads.reshape(2 * capacity, hidden_width)
    grad_pre = expert_backward(flat_in, flat_grad, matrix)
    grad_rows = lax.dot_general(
        grad_pre, matrix, (((1,), (1,)), ((), ())), preferred_element_type=jnp.float32
    )
    row_index = jnp.transpose(
        jnp.clip(slot_index, 0, capacity - 1) + (jnp.arange(2, dtype=jnp.int32) * capacity)[:, None]
    )
    routed_rows = jnp.transpose(routed)
    picked = jnp.take(grad_rows, row_index, axis=0)
    summed = lax.psum_scatter(
        jnp.where(routed_rows[..., None], picked, jnp.float32(0.0)),
        "expert",
        scatter_dimension=0,
        tiled=True,
    ).astype(jnp.bfloat16)
    from_next = from_behind(summed[:, 0], "section", -1)
    from_prior = from_behind(summed[:, 1], "section", 1)
    d_in = jnp.stack([from_next, from_prior], axis=1)[None]
    local_grad = weight_product(flat_in, grad_pre)
    half_cycle = lax.axis_size("section") // 2
    twin_grad = passed_along(local_grad, "section", half_cycle)
    summed_grad = (local_grad.astype(jnp.float32) + twin_grad.astype(jnp.float32)).astype(
        jnp.bfloat16
    )
    return (d_in, summed_grad[None, None])


def solution(mesh):
    in_specs = (
        P("section", None, None, None),
        P("section", None, "expert", None, None),
        P("section", None, "expert", None, None),
        P("section", "expert", None, None),
    )
    out_specs = (P("section", "expert", None, None), P("section", "expert", None, None))
    return jax.shard_map(body, mesh=mesh, in_specs=in_specs, out_specs=out_specs, check_vma=False)
```

profile of v0, /device:TPU:224, one launch (start us, length us, event | category | flops | bytes accessed | tf_op | source)
XLA Modules:
  0.0 127.4 jit_solution(10114619960128863601)
XLA Ops:
  7.2 0.0 copy-start
  7.2 0.0 reduce-scatter.2.cloned.1.call-start
  7.2 0.8 compare_reduce_fusion
  8.0 0.1 convert_reduce_fusion
  8.2 0.1 iota_compare_fusion
  8.3 0.1 lt.27
  8.4 0.6 reduce-window.6
  9.0 0.2 slice_reduce_fusion
  9.2 0.2 reduce-window.9
  9.4 0.1 clamp_bitcast_fusion
  9.4 0.1 compare_and_fusion
  9.5 0.1 copy.14
  9.7 0.1 reshape.57
  9.8 0.0 copy-done
  9.8 0.0 copy-start.3
  9.8 1.9 %fusion.4 = f32[384,768]{1,0:T(8,128)S(1)} fusion(bf16[384,1024]{1,0:T(8,128)(2,1)} %bitcast.44, bf16[1,1,1024,768]{3,2,1,0:T(8,128)(2,1)S(1)} %copy-done), kind=kOutput, calls=%fused_computation.8 | convolution fusion | flops 603979776 | bytes 3538944 | tf_op jit(solution)/shard_map/dot_general | solution.py:21
  11.8 0.0 copy-done.3
  11.8 0.3 fusion.9
  12.2 0.0 copy-start.2
  12.2 0.7 copy-done.2
  12.9 0.8 fusion.2
  13.7 2.7 %gather_fusion = f32[512,1024]{1,0:T(8,128)} fusion(f32[384,1024]{1,0:T(8,128)S(1)} %fusion.2, s32[1024]{0:T(1024)S(1)} %pad_clamp_fusion), kind=kCustom, calls=%fused_computation | custom fusion | bytes 4196352 | tf_op jit(solution)/shard_map/jit(_take)/gather | solution.py:60
  16.4 3.5 %reshape.56 = f32[256,2,1024]{2,1,0:T(2,128)} reshape(f32[512,1024]{1,0:T(8,128)} %gather_fusion) | data formatting | bytes 4194304 | tf_op jit(solution)/shard_map/jit(_take)/gather | solution.py:60
  19.9 3.7 %fusion = f32[256,2,1024]{2,0,1:T(8,128)} fusion(f32[256,2,1024]{2,1,0:T(2,128)} %reshape.56, pred[256,2]{0,1:T(4,128)(4,1)S(1)} %get-tuple-element.8, pred[256,2]{0,1:T(4,128)(4,1)S(1)} %bitcast.42), kind=kLoop, calls=%fused_computation.3 | loop fusion | flops 1048576 | bytes 4195328 | tf_op jit(solution)/shard_map/jit(_where)/select_n | solution.py:62
  23.6 0.0 reduce-scatter.2.cloned.1.call-update
  23.6 2.2 %fusion.6 = bf16[1024,768]{0,1:T(8,128)(2,1)S(1)} fusion(bf16[384,1024]{1,0:T(8,128)(2,1)} %bitcast.45, bf16[384,384]{1,0:T(8,128)(2,1)} %copy-done.2, bf16[384,384]{1,0:T(8,128)(2,1)S(1)} %get-tuple-element.10), kind=kOutput, calls=%fused_computation.10 | convolution fusion | flops 605945856 | bytes 2949120 | tf_op jit(solution)/shard_map/dot_general | solution.py:32
  25.8 0.0 copy-start.1
  25.8 2.0 %collective-permute-start.2 = (bf16[1024,768]{0,1:T(8,128)(2,1)S(1)}, bf16[1024,768]{0,1:T(8,128)(2,1)}, u32[]{:S(2)}, u32[]{:S(2)}) collective-permute-start(bf16[1024,768]{0,1:T(8,128)(2,1)S(1)} %fusion.6), channel_id=1, source_target_pairs={{384,0},{388,4},{392,8},{396,12},{400,16},{404,20},{408,24},{412,2... | collective-permute-start | bytes 4718600 | tf_op jit(solution)/shard_map/ppermute | solution.py:16
  27.9 74.1 %reduce-scatter.2.cloned.1.call-done = f32[64,2,1024]{2,0,1:T(8,128)} async-done(((f32[256,2,1024]{2,0,1:T(8,128)}), f32[64,2,1024]{2,0,1:T(8,128)}) %reduce-scatter.2.cloned.1.call-update) | async-done | bytes 524304 | tf_op jit(solution)/shard_map/reduce_scatter | solution.py:61
  101.9 1.1 convert_element_type.36
  103.0 0.7 slice_bitcast_fusion.1
  103.7 1.9 %collective-permute-start = (bf16[64,1024]{1,0:T(8,128)(2,1)}, bf16[64,1024]{1,0:T(8,128)(2,1)}, u32[]{:S(2)}, u32[]{:S(2)}) collective-permute-start(bf16[64,1024]{1,0:T(8,128)(2,1)} %get-tuple-element.12), channel_id=1, source_target_pairs={{4,0},{8,4},{12,8},{16,12},{20,16},{24,20},{28,24},{32,28},{36,32}... | collective-permute-start | bytes 393224 | tf_op jit(solution)/shard_map/ppermute | solution.py:10
  105.6 2.4 %collective-permute-start.1 = (bf16[64,1024]{1,0:T(8,128)(2,1)}, bf16[64,1024]{1,0:T(8,128)(2,1)}, u32[]{:S(2)}, u32[]{:S(2)}) collective-permute-start(bf16[64,1024]{1,0:T(8,128)(2,1)} %get-tuple-element.13), channel_id=1, source_target_pairs={{0,4},{4,8},{8,12},{12,16},{16,20},{20,24},{24,28},{28,32},{32,36}... | collective-permute-start | bytes 393224 | tf_op jit(solution)/shard_map/ppermute | solution.py:10
  108.1 0.0 copy-done.1
  108.1 0.0 collective-permute-done.2
  108.1 2.6 %fusion.1 = bf16[1,1,1024,768]{2,3,1,0:T(8,128)(2,1)S(1)} fusion(bf16[1024,768]{0,1:T(8,128)(2,1)} %collective-permute-done.2, bf16[1024,768]{0,1:T(8,128)(2,1)} %copy-done.1), kind=kLoop, calls=%fused_computation.5 | loop fusion | flops 3145728 | bytes 4718592 | tf_op jit(solution)/shard_map/broadcast_in_dim | solution.py:76
  110.6 1.6 %copy.17 = bf16[1,1,1024,768]{3,2,1,0:T(8,128)(2,1)} copy(bf16[1,1,1024,768]{2,3,1,0:T(8,128)(2,1)S(1)} %fusion.1) | data formatting | bytes 3145728
  112.2 0.0 collective-permute-done
  112.2 6.4 %collective-permute-done.1 = bf16[64,1024]{1,0:T(8,128)(2,1)} collective-permute-done((bf16[64,1024]{1,0:T(8,128)(2,1)}, bf16[64,1024]{1,0:T(8,128)(2,1)}, u32[]{:S(2)}, u32[]{:S(2)}) %collective-permute-start.1) | collective-permute-done | bytes 131104 | tf_op jit(solution)/shard_map/ppermute | solution.py:10
  118.6 1.0 maximum_bitcast_fusion
  119.6 1.0 copy.16
  (4 shorter events, 0.0 us)
Async XLA Ops:
  7.2 2.7 %copy-start = (bf16[1,1,1024,768]{3,2,1,0:T(8,128)(2,1)S(1)}, bf16[1,1,1024,768]{3,2,1,0:T(8,128)(2,1)}, u32[]{:S(2)}) copy-start(bf16[1,1,1024,768]{3,2,1,0:T(8,128)(2,1)} %param.7) | copy-start | bytes 4718596
  7.2 94.8 %reduce-scatter.2.cloned.1.call-start = ((), (), s32[]{:S(2)}) async-start(), calls=%async_computation.1 | async-start | bytes 2621440 | tf_op jit(solution)/shard_map/reduce_scatter | solution.py:61
  9.8 2.0 %copy-start.3 = (bf16[1,2,1,192,384]{4,3,2,1,0:T(8,128)(2,1)S(1)}, bf16[1,2,1,192,384]{4,3,2,1,0:T(8,128)(2,1)}, u32[]{:S(2)}) copy-start(bf16[1,2,1,192,384]{4,3,2,1,0:T(8,128)(2,1)} %param.6) | copy-start | bytes 884740
  12.2 0.7 copy-start.2
  25.8 82.2 %copy-start.1 = (bf16[1024,768]{0,1:T(8,128)(2,1)}, bf16[1024,768]{0,1:T(8,128)(2,1)S(1)}, u32[]{:S(2)}) copy-start(bf16[1024,768]{0,1:T(8,128)(2,1)S(1)} %fusion.6) | copy-start | bytes 4718596
  25.8 82.2 %collective-permute-start.2 = (bf16[1024,768]{0,1:T(8,128)(2,1)S(1)}, bf16[1024,768]{0,1:T(8,128)(2,1)}, u32[]{:S(2)}, u32[]{:S(2)}) collective-permute-start(bf16[1024,768]{0,1:T(8,128)(2,1)S(1)} %fusion.6), channel_id=1, source_target_pairs={{384,0},{388,4},{392,8},{396,12},{400,16},{404,20},{408,24},{412,2... | collective-permute-start | bytes 4718600 | tf_op jit(solution)/shard_map/ppermute | solution.py:16
  103.7 8.5 %collective-permute-start = (bf16[64,1024]{1,0:T(8,128)(2,1)}, bf16[64,1024]{1,0:T(8,128)(2,1)}, u32[]{:S(2)}, u32[]{:S(2)}) collective-permute-start(bf16[64,1024]{1,0:T(8,128)(2,1)} %get-tuple-element.12), channel_id=1, source_target_pairs={{4,0},{8,4},{12,8},{16,12},{20,16},{24,20},{28,24},{32,28},{36,32}... | collective-permute-start | bytes 393224 | tf_op jit(solution)/shard_map/ppermute | solution.py:10
  105.6 12.9 %collective-permute-start.1 = (bf16[64,1024]{1,0:T(8,128)(2,1)}, bf16[64,1024]{1,0:T(8,128)(2,1)}, u32[]{:S(2)}, u32[]{:S(2)}) collective-permute-start(bf16[64,1024]{1,0:T(8,128)(2,1)} %get-tuple-element.13), channel_id=1, source_target_pairs={{0,4},{4,8},{8,12},{12,16},{16,20},{20,24},{24,28},{28,32},{32,36}... | collective-permute-start | bytes 393224 | tf_op jit(solution)/shard_map/ppermute | solution.py:10
Sparse Core Ops, SparseCore 0:
  23.7 78.2 reduce-scatter.1
where the time goes:
time: 128 us; the launch traced here: 127 us
  waiting for transfers between devices  80.5 us (63%)
  between operations  14.2 us (11%)
  local copies, waits for them, and re-layouts  10.7 us (8%)
  other arithmetic  10.6 us (8%)
  starting transfers between devices  6.38 us (5%)
  matrix products  4.98 us (4%)
    reduce_scatter x1, waiting for transfers between devices, body(): lax.psum_scatter(jnp.where(routed_rows[..., None], picked, jnp.float32(0....  74.1 us
    ppermute x2, waiting for transfers between devices, from_behind(): return lax.ppermute(block, axis, route)  6.36 us
    gather x2, local copies, waits for them, and re-layouts, body(): picked = jnp.take(grad_rows, row_index, axis=0)  6.17 us
    ppermute x2, starting transfers between devices, from_behind(): return lax.ppermute(block, axis, route)  4.32 us
    select_n x1, other arithmetic, body(): jnp.where(routed_rows[..., None], picked, jnp.float32(0.0))  3.7 us
    unnamed x10, local copies, waits for them, and re-layouts  3.27 us
  transfers between devices with their start and end apart: 4, of which 2 were waited for; matrix products, arithmetic and copies ran while one was open for 6% of the time, Pallas kernels for 0%

commit v1 on v0

v1 whole, which is shorter than its diff:
```python
import jax
import jax.numpy as jnp
from jax import lax
from jax.experimental import pallas as pl
from jax.experimental.pallas import tpu as pltpu
from jax.sharding import PartitionSpec as P

MESH = pl.DeviceIdType.MESH
BF16 = jnp.bfloat16
F32 = jnp.float32


def gradients(x, h, w):
    ff = h.shape[1]
    projected = jnp.dot(x, w, preferred_element_type=F32)
    gate = projected[:, :ff]
    up = projected[:, ff:]
    sg = 1.0 / (1.0 + jnp.exp(-gate))
    hf = h.astype(F32)
    hs = hf * sg
    grad_gate = hs * up * (1.0 + gate * (1.0 - sg))
    grad_up = hs * gate
    return grad_gate.astype(BF16), grad_up.astype(BF16)


def exchange_kernel(
    routes, x_hbm, h_hbm, w_hbm,
    d_out, h_twin, local_out,
    x, h, w, g, part, far, near, mid, total, in_sems, sends, recvs,
):
    sections = lax.axis_size("section")
    experts = lax.axis_size("expert")
    s = lax.axis_index("section")
    e = lax.axis_index("expert")
    cap = x.shape[0] // 2
    ff = h.shape[1]
    toks = routes.shape[2]

    def section(step):
        return (lax.rem(s + step + sections, sections), e)

    def expert(step):
        return (s, lax.rem(e + step + experts, experts))

    up, down = expert(1), expert(-1)
    after, before = section(1), section(-1)
    twin = section(sections // 2)

    barrier = pltpu.get_barrier_semaphore()
    for partner in (twin, after, before, up, down):
        pl.semaphore_signal(barrier, inc=1, device_id=partner, device_id_type=MESH)
    loads = [
        pltpu.make_async_copy(src, dst, in_sems.at[i])
        for i, (src, dst) in enumerate(((h_hbm, h), (x_hbm, x), (w_hbm, w)))
    ]
    for load in loads:
        load.start()

    upper = (
        lax.broadcasted_iota(jnp.int32, (toks, toks), 0)
        <= lax.broadcasted_iota(jnp.int32, (toks, toks), 1)
    ).astype(F32).astype(BF16)
    slots = lax.broadcasted_iota(jnp.int32, (cap, toks), 0).astype(F32)
    one_hots, counts = [], []
    for r in range(2):
        named = routes[r]
        routed = (named[0:1] == e) | (named[1:2] == e)
        flags = jnp.where(routed, 1.0, 0.0).astype(F32)
        running = jnp.dot(
            jnp.broadcast_to(flags, (16, toks)).astype(BF16), upper, preferred_element_type=F32
        )[0:1]
        slot = jnp.where(routed, running - 1.0, -1.0)
        one_hots.append(jnp.where(slots == slot, 1.0, 0.0).astype(BF16))
        counts.append(jnp.sum(flags, axis=1, keepdims=True))

    loads[0].wait()
    live_rows = lax.broadcasted_iota(jnp.int32, (cap, ff), 0).astype(F32)
    for r in range(2):
        rows = pl.ds(r * cap, cap)
        h[rows] = jnp.where(live_rows < counts[r], h[rows], jnp.zeros((), BF16))

    loads[1].wait()
    loads[2].wait()
    for r in range(2):
        rows = pl.ds(r * cap, cap)
        grad_gate, grad_up = gradients(x[rows], h[rows], w[...])
        g[rows, :ff] = grad_gate
        g[rows, ff:] = grad_up
        ordered = lax.dot_general(
            one_hots[r], g[rows], (((0,), (0,)), ((), ())), preferred_element_type=F32
        ).astype(BF16)
        grad_rows = lax.dot_general(
            ordered, w[...], (((1,), (1,)), ((), ())), preferred_element_type=F32
        ).astype(BF16)
        part[r] = grad_rows.reshape(part.shape[1:])

    def send(i, src, dst, device):
        copy = pltpu.make_async_remote_copy(
            src_ref=src, dst_ref=dst, send_sem=sends.at[i], recv_sem=recvs.at[i],
            device_id=device, device_id_type=MESH,
        )
        copy.start()
        return copy

    pl.semaphore_wait(barrier, 5)
    far_owner = lax.rem(e + 2, experts)
    up_owner, down_owner = up[1], down[1]
    far_up = send(0, part.at[0, far_owner], far.at[0], up)
    far_down = send(1, part.at[1, far_owner], far.at[1], down)
    near_up = send(2, part.at[1, up_owner], near.at[1], up)
    near_down = send(3, part.at[0, down_owner], near.at[0], down)
    hidden = send(4, h, h_twin, twin)

    far_up.wait_recv()
    mid[0] = (part[0, up_owner].astype(F32) + far[0].astype(F32)).astype(BF16)
    far_down.wait_recv()
    mid[1] = (part[1, down_owner].astype(F32) + far[1].astype(F32)).astype(BF16)
    mid_up = send(5, mid.at[0], total.at[0], up)
    mid_down = send(6, mid.at[1], total.at[1], down)

    local_out[...] = lax.dot_general(
        x[...], g[...], (((0,), (0,)), ((), ())), preferred_element_type=F32
    ).astype(BF16)

    near_up.wait_recv()
    near_down.wait_recv()
    mid_up.wait_recv()
    mid_down.wait_recv()
    far_up.wait_send()
    far_down.wait_send()
    for r in range(2):
        far[r] = (
            part[r, e].astype(F32) + near[r].astype(F32) + total[r].astype(F32)
        ).astype(BF16)
    to_before = send(7, far.at[0], d_out.at[0], before)
    to_after = send(8, far.at[1], d_out.at[1], after)
    for copy in (near_up, near_down, mid_up, mid_down):
        copy.wait_send()
    hidden.wait()
    to_before.wait()
    to_after.wait()


def exchange(routes, x, h, w, toks_owned):
    width = x.shape[1]
    hbm = pl.BlockSpec(memory_space=pl.ANY)
    vmem = pl.BlockSpec(memory_space=pltpu.VMEM)
    block = (2, toks_owned, width)
    return pl.pallas_call(
        exchange_kernel,
        name="exchange",
        out_shape=(
            jax.ShapeDtypeStruct(block, BF16),
            jax.ShapeDtypeStruct(h.shape, BF16),
            jax.ShapeDtypeStruct(w.shape, BF16),
        ),
        in_specs=[vmem, hbm, hbm, hbm],
        out_specs=(hbm, hbm, vmem),
        scratch_shapes=[
            pltpu.VMEM(x.shape, BF16),
            pltpu.VMEM(h.shape, BF16),
            pltpu.VMEM(w.shape, BF16),
            pltpu.VMEM((x.shape[0], w.shape[1]), BF16),
            pltpu.VMEM((2, routes.shape[2] // toks_owned, toks_owned, width), BF16),
            pltpu.VMEM(block, BF16),
            pltpu.VMEM(block, BF16),
            pltpu.VMEM(block, BF16),
            pltpu.VMEM(block, BF16),
            pltpu.SemaphoreType.DMA((3,)),
            pltpu.SemaphoreType.DMA((9,)),
            pltpu.SemaphoreType.DMA((9,)),
        ],
        compiler_params=pltpu.CompilerParams(collective_id=0, has_side_effects=True),
        cost_estimate=pl.CostEstimate(
            flops=2_000_000_000, bytes_accessed=8_000_000, transcendentals=150_000
        ),
    )(routes, x, h, w)


def twin_kernel(x, h, w, local, out, g):
    tile = out.shape[0]
    step = pl.program_id(0)

    @pl.when(step == 0)
    def _():
        ff = h.shape[1]
        grad_gate, grad_up = gradients(x[...], h[...], w[...])
        g[:, :ff] = grad_gate
        g[:, ff:] = grad_up

    columns = pl.ds(pl.multiple_of(step * tile, tile), tile)
    product = lax.dot_general(
        x[:, columns], g[...], (((0,), (0,)), ((), ())), preferred_element_type=F32
    )
    out[...] = (local[...].astype(F32) + product).astype(BF16)


def weight_sum(x, h, w, local):
    tile = 256
    whole = lambda a: pl.BlockSpec(a.shape, lambda i: (0, 0), pipeline_mode=pl.Buffered(1))
    rows = pl.BlockSpec((tile, w.shape[1]), lambda i: (i, 0))
    resident = pl.BlockSpec(memory_space=pltpu.VMEM)
    return pl.pallas_call(
        twin_kernel,
        name="twin_product",
        grid=(w.shape[0] // tile,),
        out_shape=jax.ShapeDtypeStruct(w.shape, BF16),
        in_specs=[resident, whole(h), whole(w), rows],
        out_specs=rows,
        scratch_shapes=[pltpu.VMEM((x.shape[0], w.shape[1]), BF16)],
        cost_estimate=pl.CostEstimate(
            flops=1_200_000_000, bytes_accessed=5_700_000, transcendentals=150_000
        ),
    )(x, h, w, local)


def body(routes, x_blocks, d_hidden, weights):
    sections = lax.axis_size("section")
    experts = lax.axis_size("expert")
    s = lax.axis_index("section")
    named = jnp.transpose(routes[0], (0, 2, 1))
    x = x_blocks.reshape(-1, x_blocks.shape[4])
    h = d_hidden.reshape(-1, d_hidden.shape[4])
    w = weights[0, 0]
    half = sections // 2
    x_twin = lax.ppermute(x, "section", [((i + half) % sections, i) for i in range(sections)])
    pair, h_twin, local = exchange(named, x, h, w, named.shape[2] // experts)
    zero = jnp.zeros((), BF16)
    d_in = jnp.stack(
        [jnp.where(s == sections - 1, zero, pair[0]), jnp.where(s == 0, zero, pair[1])], axis=1
    )
    d_weights = weight_sum(x_twin, h_twin, w, local)
    return (d_in[None], d_weights[None, None])


def solution(mesh):
    in_specs = (
        P("section", None, None, None),
        P("section", None, "expert", None, None),
        P("section", None, "expert", None, None),
        P("section", "expert", None, None),
    )
    out_specs = (P("section", "expert", None, None), P("section", "expert", None, None))
    return jax.shard_map(body, mesh=mesh, in_specs=in_specs, out_specs=out_specs, check_vma=False)
```

time: 128 us -> 68.6 us (0.54)
  the two profiles are of different devices: /device:TPU:224 before, /device:TPU:1 now
where the time goes in v1:
time: 68.6 us; the launch traced here: 68 us
  Pallas kernels  56.1 us (82%)
  starting transfers between devices  8.27 us (12%)
  local copies, waits for them, and re-layouts  1.88 us (3%)
  other arithmetic  1.02 us (1%)
    pallas_call x1, Pallas kernels, exchange(): pl.pallas_call(exchange_kernel, name='exchange', out_shape=(jax.ShapeDtyp...  50.1 us
    ppermute x1, starting transfers between devices, body(): lax.ppermute(x, 'section', [((i + half) % sections, i) for i in range(sec...  8.27 us
    pallas_call x1, Pallas kernels, weight_sum(): pl.pallas_call(twin_kernel, name='twin_product', grid=(w.shape[0] // tile...  6.04 us
    unnamed x3, local copies, waits for them, and re-layouts  1.88 us
  transfers between devices with their start and end apart: 1, of which 0 were waited for; matrix products, arithmetic and copies ran while one was open for 3% of the time, Pallas kernels for 74%

profile of v1, /device:TPU:1, one launch (start us, length us, event | category | flops | bytes accessed | tf_op | source)
XLA Modules:
  0.0 68.0 jit_solution(7424397432536470721)
XLA Ops:
  0.6 8.3 %collective-permute-start = (bf16[384,1024]{1,0:T(8,128)(2,1)}, bf16[384,1024]{1,0:T(8,128)(2,1)S(1)}, u32[]{:S(2)}, u32[]{:S(2)}) collective-permute-start(bf16[384,1024]{1,0:T(8,128)(2,1)} %bitcast.16), channel_id=1, source_target_pairs={{384,0},{388,4},{392,8},{396,12},{400,16},{404,20},{408,24},{412,2... | collective-permute-start | bytes 2359304 | tf_op jit(solution)/shard_map/ppermute | solution.py:226
  8.9 50.1 %exchange.1 = (bf16[2,64,1024]{2,1,0:T(8,128)(2,1)}, bf16[384,384]{1,0:T(8,128)(2,1)}, bf16[1024,768]{1,0:T(8,128)(2,1)}) custom-call(s32[2,2,256]{2,1,0:T(2,128)} %bitcast.19, bf16[384,1024]{1,0:T(8,128)(2,1)} %bitcast.17, bf16[384,384]{1,0:T(8,128)(2,1)} %bitcast.18, bf16[1024,768]{1,0:T(8,128)(2,1)} %bitcast.13), custom_call_target="tpu_custom_call" | custom-call | flops 2000000000 | bytes 8000000 | tf_op jit(solution)/shard_map/exchange/pallas_call | solution.py:149
  59.0 1.0 %select_bitcast_fusion.1 = (bf16[64,1,1024]{2,0,1:T(8,128)(2,1)S(1)}, bf16[64,1,1024]{2,0,1:T(8,128)(2,1)S(1)}) fusion(bf16[2,64,1024]{2,1,0:T(8,128)(2,1)} %get-tuple-element.5, pred[]{:T(512)S(6)} %eq.6, pred[]{:T(512)S(6)} %eq.7), kind=kLoop, calls=%fused_computation.2 | loop fusion | flops 131072 | bytes 524290 | tf_op jit(solution)/shard_map/jit(_where)/select_n | solution.py:230
  60.0 1.0 %copy.6 = bf16[1,64,2,1024]{3,2,1,0:T(2,128)(2,1)} copy(bf16[1,64,2,1024]{3,1,2,0:T(8,128)(2,1)S(1)} %maximum_bitcast_fusion) | data formatting | bytes 524288
  61.0 0.0 collective-permute-done.x
  61.0 0.0 copy-start
  61.0 0.9 %copy-done = bf16[384,1024]{1,0:T(8,128)(2,1)} copy-done((bf16[384,1024]{1,0:T(8,128)(2,1)}, bf16[384,1024]{1,0:T(8,128)(2,1)S(1)}, u32[]{:S(2)}) %copy-start) | copy-done | bytes 786456
  61.9 6.0 %twin_product.1 = bf16[1024,768]{1,0:T(8,128)(2,1)} custom-call(bf16[384,1024]{1,0:T(8,128)(2,1)} %copy-done, bf16[384,384]{1,0:T(8,128)(2,1)} %get-tuple-element.6.h, bf16[1024,768]{1,0:T(8,128)(2,1)} %bitcast.14, bf16[1024,768]{1,0:T(8,128)(2,1)} %get-tuple-element.7.local), custom_call_target="tpu_custom_call" | custom-call | flops 1200000000 | bytes 5700000 | tf_op jit(solution)/shard_map/twin_product/pallas_call | solution.py:203
  (1 shorter events, 0.0 us)
Async XLA Ops:
  0.6 60.4 %collective-permute-start = (bf16[384,1024]{1,0:T(8,128)(2,1)}, bf16[384,1024]{1,0:T(8,128)(2,1)S(1)}, u32[]{:S(2)}, u32[]{:S(2)}) collective-permute-start(bf16[384,1024]{1,0:T(8,128)(2,1)} %bitcast.16), channel_id=1, source_target_pairs={{384,0},{388,4},{392,8},{396,12},{400,16},{404,20},{408,24},{412,2... | collective-permute-start | bytes 2359304 | tf_op jit(solution)/shard_map/ppermute | solution.py:226
  61.0 0.9 %copy-start = (bf16[384,1024]{1,0:T(8,128)(2,1)}, bf16[384,1024]{1,0:T(8,128)(2,1)S(1)}, u32[]{:S(2)}) copy-start(bf16[384,1024]{1,0:T(8,128)(2,1)S(1)} %collective-permute-done.x) | copy-start | bytes 2359300

commit v2 on v1

v2 whole, which is shorter than its diff:
```python
import jax
import jax.numpy as jnp
from jax import lax
from jax.experimental import pallas as pl
from jax.experimental.pallas import tpu as pltpu
from jax.sharding import PartitionSpec as P

MESH = pl.DeviceIdType.MESH
BF16 = jnp.bfloat16
F32 = jnp.float32


def gradients(x, h, w):
    ff = h.shape[1]
    projected = jnp.dot(x, w, preferred_element_type=F32)
    gate = projected[:, :ff]
    up = projected[:, ff:]
    sg = 1.0 / (1.0 + jnp.exp(-gate))
    hf = h.astype(F32)
    hs = hf * sg
    grad_gate = hs * up * (1.0 + gate * (1.0 - sg))
    grad_up = hs * gate
    return grad_gate.astype(BF16), grad_up.astype(BF16)


def exchange_kernel(
    routes, x_hbm, h_hbm, w_hbm,
    d_out, most_out, x_last, h_last, w,
    x, h, g, part, far, near, mid, total, x_twin, h_twin, g_twin, acc,
    named_rows, in_sems, sends, recvs, ready,
):
    sections = lax.axis_size("section")
    experts = lax.axis_size("expert")
    s = lax.axis_index("section")
    e = lax.axis_index("expert")
    cap = x.shape[0] // 2
    ff = h.shape[1]
    toks = named_rows.shape[2]
    half = sections // 2
    core = lax.rem(s, 2)

    def section(step):
        return (lax.rem(s + step + sections, sections), e)

    def expert(step):
        return (s, lax.rem(e + step + experts, experts))

    up, down = expert(1), expert(-1)
    after, before = section(1), section(-1)
    twin = section(half)
    mate = (s + 1 - 2 * core, e)

    barrier = pltpu.get_barrier_semaphore()

    def greet(device):
        pl.semaphore_signal(barrier, inc=1, device_id=device, device_id_type=MESH)

    even = s - core
    greet((lax.rem(even + half, sections), e))

    @pl.when(core == 1)
    def _():
        greet(mate)

    odd = even + 1
    greet((odd, up[1]))
    greet((odd, down[1]))
    greet((lax.rem(odd + 2 - 4 * (1 - core) + sections, sections), e))

    loads = [
        pltpu.make_async_copy(src, dst, in_sems.at[i])
        for i, (src, dst) in enumerate(((routes, named_rows), (h_hbm, h), (x_hbm, x), (w_hbm, w)))
    ]
    for load in loads:
        load.start()

    loads[0].wait()
    upper = (
        lax.broadcasted_iota(jnp.int32, (toks, toks), 0)
        <= lax.broadcasted_iota(jnp.int32, (toks, toks), 1)
    ).astype(F32).astype(BF16)
    slots = lax.broadcasted_iota(jnp.int32, (cap, toks), 0).astype(F32)
    one_hots, counts = [], []
    for r in range(2):
        named = named_rows[r]
        routed = (named[0:1] == e) | (named[1:2] == e)
        flags = jnp.where(routed, 1.0, 0.0).astype(F32)
        running = jnp.dot(
            jnp.broadcast_to(flags, (16, toks)).astype(BF16), upper, preferred_element_type=F32
        )[0:1]
        slot = jnp.where(routed, running - 1.0, -1.0)
        one_hots.append(jnp.where(slots == slot, 1.0, 0.0).astype(BF16))
        counts.append(jnp.sum(flags, axis=1, keepdims=True))

    loads[1].wait()
    live_rows = lax.broadcasted_iota(jnp.int32, (cap, ff), 0).astype(F32)
    for r in range(2):
        rows = pl.ds(r * cap, cap)
        h[rows] = jnp.where(live_rows < counts[r], h[rows], jnp.zeros((), BF16))

    @pl.when(core == 0)
    def _():
        pl.semaphore_wait(barrier, 3)
        pl.semaphore_signal(ready, inc=1, device_id=mate, device_id_type=MESH)

    @pl.when(core == 1)
    def _():
        pl.semaphore_wait(ready, 1)

    def send(i, src, dst, device):
        copy = pltpu.make_async_remote_copy(
            src_ref=src, dst_ref=dst, send_sem=sends.at[i], recv_sem=recvs.at[i],
            device_id=device, device_id_type=MESH,
        )
        copy.start()
        return copy

    kept = x_twin.shape[0]
    first = cap
    to_twin = [
        send(8, h.at[pl.ds(0, kept)], h_twin, twin),
        send(9, x_hbm.at[pl.ds(0, first)], x_twin.at[pl.ds(0, first)], twin),
        send(10, x_hbm.at[pl.ds(first, kept - first)], x_twin.at[pl.ds(first, kept - first)], twin),
        send(11, h.at[pl.ds(kept, x_last.shape[0])], h_last, twin),
        send(12, x_hbm.at[pl.ds(kept, x_last.shape[0])], x_last, twin),
    ]

    loads[2].wait()
    loads[3].wait()
    for r in range(2):
        rows = pl.ds(r * cap, cap)
        grad_gate, grad_up = gradients(x[rows], h[rows], w[...])
        g[rows, :ff] = grad_gate
        g[rows, ff:] = grad_up
        ordered = lax.dot_general(
            one_hots[r], g[rows], (((0,), (0,)), ((), ())), preferred_element_type=F32
        ).astype(BF16)
        grad_rows = lax.dot_general(
            ordered, w[...], (((1,), (1,)), ((), ())), preferred_element_type=F32
        ).astype(BF16)
        part[r] = grad_rows.reshape(part.shape[1:])

    @pl.when(core == 1)
    def _():
        pl.semaphore_wait(barrier, 6)
        pl.semaphore_signal(ready, inc=1, device_id=mate, device_id_type=MESH)

    @pl.when(core == 0)
    def _():
        pl.semaphore_wait(ready, 1)

    far_owner = lax.rem(e + 2, experts)
    up_owner, down_owner = up[1], down[1]
    far_up = send(0, part.at[0, far_owner], far.at[0], up)
    far_down = send(1, part.at[1, far_owner], far.at[1], down)
    near_up = send(2, part.at[1, up_owner], near.at[1], up)
    near_down = send(3, part.at[0, down_owner], near.at[0], down)

    acc[...] = lax.dot_general(
        x[...], g[...], (((0,), (0,)), ((), ())), preferred_element_type=F32
    )

    far_up.wait_recv()
    mid[0] = (part[0, up_owner].astype(F32) + far[0].astype(F32)).astype(BF16)
    mid_up = send(4, mid.at[0], total.at[0], up)
    far_down.wait_recv()
    mid[1] = (part[1, down_owner].astype(F32) + far[1].astype(F32)).astype(BF16)
    mid_down = send(5, mid.at[1], total.at[1], down)

    def twin_chunk(start, count):
        rows = pl.ds(start, count)
        grad_gate, grad_up = gradients(x_twin[rows], h_twin[rows], w[...])
        g_twin[rows, :ff] = grad_gate
        g_twin[rows, ff:] = grad_up
        return lax.dot_general(
            x_twin[rows], g_twin[rows], (((0,), (0,)), ((), ())), preferred_element_type=F32
        )

    to_twin[0].wait_recv()
    to_twin[1].wait_recv()
    acc[...] += twin_chunk(0, first)

    near_up.wait_recv()
    near_down.wait_recv()
    mid_up.wait_recv()
    mid_down.wait_recv()
    far_up.wait_send()
    far_down.wait_send()
    for r in range(2):
        far[r] = (
            part[r, e].astype(F32) + near[r].astype(F32) + total[r].astype(F32)
        ).astype(BF16)
    to_before = send(6, far.at[0], d_out.at[0], before)
    to_after = send(7, far.at[1], d_out.at[1], after)

    to_twin[2].wait_recv()
    most_out[...] = (acc[...] + twin_chunk(first, kept - first)).astype(BF16)

    for copy in (near_up, near_down, mid_up, mid_down):
        copy.wait_send()
    to_before.wait()
    to_after.wait()
    for copy in to_twin:
        copy.wait_send()
    to_twin[3].wait_recv()
    to_twin[4].wait_recv()


def exchange(routes, x, h, w, toks_owned, kept):
    width = x.shape[1]
    hbm = pl.BlockSpec(memory_space=pltpu.HBM)
    anywhere = pl.BlockSpec(memory_space=pl.ANY)
    vmem = pl.BlockSpec(memory_space=pltpu.VMEM)
    block = (2, toks_owned, width)
    left = x.shape[0] - kept
    return pl.pallas_call(
        exchange_kernel,
        name="exchange",
        out_shape=(
            jax.ShapeDtypeStruct(block, BF16),
            jax.ShapeDtypeStruct(w.shape, BF16),
            jax.ShapeDtypeStruct((left, width), BF16),
            jax.ShapeDtypeStruct((left, h.shape[1]), BF16),
            jax.ShapeDtypeStruct(w.shape, BF16),
        ),
        in_specs=[hbm, hbm, hbm, hbm],
        out_specs=(anywhere, vmem, anywhere, anywhere, vmem),
        scratch_shapes=[
            pltpu.VMEM(x.shape, BF16),
            pltpu.VMEM(h.shape, BF16),
            pltpu.VMEM((x.shape[0], w.shape[1]), BF16),
            pltpu.VMEM((2, routes.shape[2] // toks_owned, toks_owned, width), BF16),
            pltpu.VMEM(block, BF16),
            pltpu.VMEM(block, BF16),
            pltpu.VMEM(block, BF16),
            pltpu.VMEM(block, BF16),
            pltpu.VMEM((kept, width), BF16),
            pltpu.VMEM((kept, h.shape[1]), BF16),
            pltpu.VMEM((kept, w.shape[1]), BF16),
            pltpu.VMEM(w.shape, F32),
            pltpu.VMEM(routes.shape, jnp.int32),
            pltpu.SemaphoreType.DMA((4,)),
            pltpu.SemaphoreType.DMA((13,)),
            pltpu.SemaphoreType.DMA((13,)),
            pltpu.SemaphoreType.REGULAR,
        ],
        compiler_params=pltpu.CompilerParams(
            collective_id=0, has_side_effects=True, vmem_limit_bytes=40 * 2**20
        ),
        cost_estimate=pl.CostEstimate(
            flops=3_000_000_000, bytes_accessed=8_000_000, transcendentals=300_000
        ),
    )(*(pltpu.with_memory_space_constraint(a, pltpu.HBM) for a in (routes, x, h, w)))


def twin_kernel(x, h, w, local, out, g):
    tile = out.shape[0]
    step = pl.program_id(0)

    @pl.when(step == 0)
    def _():
        ff = h.shape[1]
        grad_gate, grad_up = gradients(x[...], h[...], w[...])
        g[:, :ff] = grad_gate
        g[:, ff:] = grad_up

    columns = pl.ds(pl.multiple_of(step * tile, tile), tile)
    product = lax.dot_general(
        x[:, columns], g[...], (((0,), (0,)), ((), ())), preferred_element_type=F32
    )
    out[...] = (local[...].astype(F32) + product).astype(BF16)


def weight_sum(x, h, w, earlier):
    tile = 256
    whole = pl.BlockSpec(memory_space=pltpu.VMEM)
    rows = pl.BlockSpec((tile, w.shape[1]), lambda i: (i, 0))
    count = x.shape[0]
    return pl.pallas_call(
        twin_kernel,
        name="twin_product",
        grid=(w.shape[0] // tile,),
        out_shape=jax.ShapeDtypeStruct(w.shape, BF16),
        in_specs=[whole, whole, whole, rows],
        out_specs=rows,
        scratch_shapes=[pltpu.VMEM((count, w.shape[1]), BF16)],
        compiler_params=pltpu.CompilerParams(vmem_limit_bytes=16 * 2**20),
        cost_estimate=pl.CostEstimate(
            flops=4 * count * w.size, bytes_accessed=5_000_000, transcendentals=count * h.shape[1]
        ),
    )(x, h, w, earlier)


def body(routes, x_blocks, d_hidden, weights):
    sections = lax.axis_size("section")
    experts = lax.axis_size("expert")
    s = lax.axis_index("section")
    named = jnp.transpose(routes[0], (0, 2, 1))
    x = x_blocks.reshape(-1, x_blocks.shape[4])
    h = d_hidden.reshape(-1, d_hidden.shape[4])
    w = weights[0, 0]
    kept = x.shape[0] * 3 // 4
    pair, most, x_last, h_last, w_held = exchange(named, x, h, w, named.shape[2] // experts, kept)
    zero = jnp.zeros((), BF16)
    d_in = jnp.stack(
        [jnp.where(s == sections - 1, zero, pair[0]), jnp.where(s == 0, zero, pair[1])], axis=1
    )
    d_weights = weight_sum(x_last, h_last, w_held, most)
    return (d_in[None], d_weights[None, None])


def solution(mesh):
    in_specs = (
        P("section", None, None, None),
        P("section", None, "expert", None, None),
        P("section", None, "expert", None, None),
        P("section", "expert", None, None),
    )
    out_specs = (P("section", "expert", None, None), P("section", "expert", None, None))
    return jax.shard_map(body, mesh=mesh, in_specs=in_specs, out_specs=out_specs, check_vma=False)
```

time: 68.6 us -> 64.1 us (0.934)
  starting transfers between devices: 8.27 us -> 0 us
  Pallas kernels: 56.1 us -> 62.2 us
  other arithmetic: 1.02 us -> 0.05 us
  local copies, waits for them, and re-layouts: 1.88 us -> 0.97 us
    pallas_call x1, Pallas kernels: 50.1 us -> 59.4 us  [exchange(): pl.pallas_call(exchange_kernel, name='exchange', out_shape=(jax.ShapeDtyp...]
    ppermute x1 -> x0, starting transfers between devices: 8.27 us -> none  [body(): lax.ppermute(x, 'section', [((i + half) % sections, i) for i in range(sec...]
    pallas_call x1, Pallas kernels: 6.04 us -> 2.8 us  [weight_sum(): pl.pallas_call(twin_kernel, name='twin_product', grid=(w.shape[0] // tile...]
    select_n x1, other arithmetic: 0.99 us -> 0.02 us  [body(): jnp.where(s == sections - 1, zero, pair[0])]
    unnamed x3 -> x1, local copies, waits for them, and re-layouts: 1.88 us -> 0.97 us
  transfers between devices with their start and end apart: 1 -> 0, of which waited for: 0 -> 0; matrix products, arithmetic and copies ran while one was open for 3% -> 0% of each run, Pallas kernels for 74% -> 0%
where the time goes in v2:
time: 64.1 us; the launch traced here: 63.9 us
  Pallas kernels  62.2 us (97%)
  local copies, waits for them, and re-layouts  0.97 us (2%)
  between operations  0.67 us (1%)
    pallas_call x1, Pallas kernels, exchange(): pl.pallas_call(exchange_kernel, name='exchange', out_shape=(jax.ShapeDtyp...  59.4 us
    pallas_call x1, Pallas kernels, weight_sum(): pl.pallas_call(twin_kernel, name='twin_product', grid=(w.shape[0] // tile...  2.8 us

profile of v2, /device:TPU:1, one launch (start us, length us, event | category | flops | bytes accessed | tf_op | source)
XLA Modules:
  0.0 63.9 jit_solution(12672936162740882187)
XLA Ops:
  0.6 59.4 %exchange.1 = (bf16[2,64,1024]{2,1,0:T(8,128)(2,1)S(1)}, bf16[1024,768]{1,0:T(8,128)(2,1)S(1)}, bf16[96,1024]{1,0:T(8,128)(2,1)S(1)}, bf16[96,384]{1,0:T(8,128)(2,1)S(1)}, bf16[1024,768]{1,0:T(8,128)(2,1)S(1)}) custom-call(s32[2,2,256]{2,1,0:T(2,128)} %bitcast.17, bf16[384,1024]{1,0:T(8,128)(2,1)} %bitcast.15, bf16[384,384]{1,0:T(8,128)(2,1)} %bitcast.16, ...), custom_call_target="tpu_custom_call" | custom-call | flops 3000000000 | bytes 8000000 | tf_op jit(solution)/shard_map/exchange/pallas_call | solution.py:216
  60.1 1.0 %copy.6 = bf16[1,64,2,1024]{3,2,1,0:T(2,128)(2,1)} copy(bf16[1,64,2,1024]{3,1,2,0:T(8,128)(2,1)S(1)} %maximum_bitcast_fusion) | data formatting | bytes 524288
  61.1 2.8 %twin_product.1 = bf16[1024,768]{1,0:T(8,128)(2,1)} custom-call(bf16[96,1024]{1,0:T(8,128)(2,1)S(1)} %get-tuple-element.8.x, bf16[96,384]{1,0:T(8,128)(2,1)S(1)} %get-tuple-element.9.h, bf16[1024,768]{1,0:T(8,128)(2,1)S(1)} %get-tuple-element.10.w, bf16[1024,768]{1,0:T(8,128)(2,1)S(1)} %get-tuple-element.11.local), custom_call_target="tpu_custom_call" | custom-call | flops 301989888 | bytes 5000000 | tf_op jit(solution)/shard_map/twin_product/pallas_call | solution.py:279
  (2 shorter events, 0.1 us)

commit v3 on v2

--- a/solution.py
+++ b/solution.py
@@ -10,23 +10,23 @@
 F32 = jnp.float32
 
 
-def gradients(x, h, w):
-    ff = h.shape[1]
+def factors(x, w):
+    ff = w.shape[1] // 2
     projected = jnp.dot(x, w, preferred_element_type=F32)
     gate = projected[:, :ff]
-    up = projected[:, ff:]
     sg = 1.0 / (1.0 + jnp.exp(-gate))
+    return projected[:, ff:], sg * (1.0 + gate * (1.0 - sg)), gate * sg
+
+
+def gradients(h, up, for_gate, for_up):
     hf = h.astype(F32)
-    hs = hf * sg
-    grad_gate = hs * up * (1.0 + gate * (1.0 - sg))
-    grad_up = hs * gate
-    return grad_gate.astype(BF16), grad_up.astype(BF16)
+    return (hf * up * for_gate).astype(BF16), (hf * for_up).astype(BF16)
 
 
 def exchange_kernel(
     routes, x_hbm, h_hbm, w_hbm,
-    d_out, most_out, x_last, h_last, w,
-    x, h, g, part, far, near, mid, total, x_twin, h_twin, g_twin, acc,
+    d_out, most_out, x_last, h_last, last_factors,
+    x, h, w, g, part, far, near, mid, total, x_twin, h_twin, g_twin, acc,
     named_rows, in_sems, sends, recvs, ready,
 ):
     sections = lax.axis_size("section")
@@ -50,22 +50,31 @@
     twin = section(half)
     mate = (s + 1 - 2 * core, e)
 
+    def is_collector(section_index):
+        return lax.rem(section_index, 2) != section_index // half
+
+    collects = is_collector(s)
     barrier = pltpu.get_barrier_semaphore()
 
     def greet(device):
         pl.semaphore_signal(barrier, inc=1, device_id=device, device_id_type=MESH)
 
-    even = s - core
-    greet((lax.rem(even + half, sections), e))
-
-    @pl.when(core == 1)
+    def collector_at(device):
+        index = device[0]
+        other = index + 1 - 2 * lax.rem(index, 2)
+        return (jnp.where(is_collector(index), index, other), device[1])
+
+    @pl.when(collects)
+    def _():
+        greet(twin)
+
+    @pl.when(jnp.logical_not(collects))
     def _():
         greet(mate)
 
-    odd = even + 1
-    greet((odd, up[1]))
-    greet((odd, down[1]))
-    greet((lax.rem(odd + 2 - 4 * (1 - core) + sections, sections), e))
+    outer = section(2 * core - 1)
+    for neighbour in (up, down, outer):
+        greet(collector_at(neighbour))
 
     loads = [
         pltpu.make_async_copy(src, dst, in_sems.at[i])
@@ -98,12 +107,12 @@
         rows = pl.ds(r * cap, cap)
         h[rows] = jnp.where(live_rows < counts[r], h[rows], jnp.zeros((), BF16))
 
-    @pl.when(core == 0)
-    def _():
-        pl.semaphore_wait(barrier, 3)
-        pl.semaphore_signal(ready, inc=1, device_id=mate, device_id_type=MESH)
-
-    @pl.when(core == 1)
+    @pl.when(jnp.logical_not(collects))
+    def _():
+        pl.semaphore_wait(barrier, 1)
+        pl.semaphore_signal(ready, inc=1, device_id=twin, device_id_type=MESH)
+
+    @pl.when(collects)
     def _():
         pl.semaphore_wait(ready, 1)
 
@@ -117,19 +126,22 @@
 
     kept = x_twin.shape[0]
     first = cap
+    kept, left = x_twin.shape[0], x_last.shape[0]
+    first = cap
+    head, middle, tail = pl.ds(0, first), pl.ds(first, kept - first), pl.ds(kept, left)
     to_twin = [
-        send(8, h.at[pl.ds(0, kept)], h_twin, twin),
-        send(9, x_hbm.at[pl.ds(0, first)], x_twin.at[pl.ds(0, first)], twin),
-        send(10, x_hbm.at[pl.ds(first, kept - first)], x_twin.at[pl.ds(first, kept - first)], twin),
-        send(11, h.at[pl.ds(kept, x_last.shape[0])], h_last, twin),
-        send(12, x_hbm.at[pl.ds(kept, x_last.shape[0])], x_last, twin),
+        send(8, x_hbm.at[head], x_twin.at[head], twin),
+        send(9, h.at[pl.ds(0, kept)], h_twin, twin),
+        send(10, x_hbm.at[middle], x_twin.at[middle], twin),
+        send(11, x_hbm.at[tail], x_last, twin),
+        send(12, h.at[tail], h_last, twin),
     ]
 
     loads[2].wait()
     loads[3].wait()
     for r in range(2):
         rows = pl.ds(r * cap, cap)
-        grad_gate, grad_up = gradients(x[rows], h[rows], w[...])
+        grad_gate, grad_up = gradients(h[rows], *factors(x[rows], w[...]))
         g[rows, :ff] = grad_gate
         g[rows, ff:] = grad_up
         ordered = lax.dot_general(
@@ -140,12 +152,12 @@
         ).astype(BF16)
         part[r] = grad_rows.reshape(part.shape[1:])
 
-    @pl.when(core == 1)
-    def _():
-        pl.semaphore_wait(barrier, 6)
+    @pl.when(collects)
+    def _():
+        pl.semaphore_wait(barrier, 7)
         pl.semaphore_signal(ready, inc=1, device_id=mate, device_id_type=MESH)
 
-    @pl.when(core == 0)
+    @pl.when(jnp.logical_not(collects))
     def _():
         pl.semaphore_wait(ready, 1)
 
@@ -169,7 +181,7 @@
 
     def twin_chunk(start, count):
         rows = pl.ds(start, count)
-        grad_gate, grad_up = gradients(x_twin[rows], h_twin[rows], w[...])
+        grad_gate, grad_up = gradients(h_twin[rows], *factors(x_twin[rows], w[...]))
         g_twin[rows, :ff] = grad_gate
         g_twin[rows, ff:] = grad_up
         return lax.dot_general(
@@ -187,22 +199,24 @@
     far_up.wait_send()
     far_down.wait_send()
     for r in range(2):
-        far[r] = (
-            part[r, e].astype(F32) + near[r].astype(F32) + total[r].astype(F32)
-        ).astype(BF16)
+        summed = part[r, e].astype(F32) + near[r].astype(F32) + total[r].astype(F32)
+        edge = s == (0 if r == 0 else sections - 1)
+        far[r] = jnp.where(edge, 0.0, summed).astype(BF16)
     to_before = send(6, far.at[0], d_out.at[0], before)
     to_after = send(7, far.at[1], d_out.at[1], after)
 
     to_twin[2].wait_recv()
     most_out[...] = (acc[...] + twin_chunk(first, kept - first)).astype(BF16)
 
+    to_twin[3].wait_recv()
+    for i, factor in enumerate(factors(x_last[...], w[...])):
+        last_factors[i] = factor
     for copy in (near_up, near_down, mid_up, mid_down):
         copy.wait_send()
     to_before.wait()
     to_after.wait()
     for copy in to_twin:
         copy.wait_send()
-    to_twin[3].wait_recv()
     to_twin[4].wait_recv()
 
 
@@ -221,13 +235,14 @@
             jax.ShapeDtypeStruct(w.shape, BF16),
             jax.ShapeDtypeStruct((left, width), BF16),
             jax.ShapeDtypeStruct((left, h.shape[1]), BF16),
-            jax.ShapeDtypeStruct(w.shape, BF16),
+            jax.ShapeDtypeStruct((3, left, h.shape[1]), F32),
         ),
         in_specs=[hbm, hbm, hbm, hbm],
-        out_specs=(anywhere, vmem, anywhere, anywhere, vmem),
+        out_specs=(anywhere, vmem, vmem, anywhere, vmem),
         scratch_shapes=[
             pltpu.VMEM(x.shape, BF16),
             pltpu.VMEM(h.shape, BF16),
+            pltpu.VMEM(w.shape, BF16),
             pltpu.VMEM((x.shape[0], w.shape[1]), BF16),
             pltpu.VMEM((2, routes.shape[2] // toks_owned, toks_owned, width), BF16),
             pltpu.VMEM(block, BF16),
@@ -253,14 +268,14 @@
     )(*(pltpu.with_memory_space_constraint(a, pltpu.HBM) for a in (routes, x, h, w)))
 
 
-def twin_kernel(x, h, w, local, out, g):
-    tile = out.shape[0]
+def last_kernel(x, h, ready_factors, earlier, pair, d_weights, d_in, g):
+    tile = d_weights.shape[0]
     step = pl.program_id(0)
 
     @pl.when(step == 0)
     def _():
         ff = h.shape[1]
-        grad_gate, grad_up = gradients(x[...], h[...], w[...])
+        grad_gate, grad_up = gradients(h[...], *(ready_factors[i] for i in range(3)))
         g[:, :ff] = grad_gate
         g[:, ff:] = grad_up
 
@@ -268,44 +283,49 @@
     product = lax.dot_general(
         x[:, columns], g[...], (((0,), (0,)), ((), ())), preferred_element_type=F32
     )
-    out[...] = (local[...].astype(F32) + product).astype(BF16)
-
-
-def weight_sum(x, h, w, earlier):
-    tile = 256
+    d_weights[...] = (earlier[...].astype(F32) + product).astype(BF16)
+    for r in range(2):
+        d_in[:, r, :] = pair[r]
+
+
+def finish(x, h, ready_factors, earlier, pair):
+    steps = 4
+    toks, width = pair.shape[1:]
     whole = pl.BlockSpec(memory_space=pltpu.VMEM)
-    rows = pl.BlockSpec((tile, w.shape[1]), lambda i: (i, 0))
+    rows = pl.BlockSpec((earlier.shape[0] // steps, earlier.shape[1]), lambda i: (i, 0))
     count = x.shape[0]
     return pl.pallas_call(
-        twin_kernel,
-        name="twin_product",
-        grid=(w.shape[0] // tile,),
-        out_shape=jax.ShapeDtypeStruct(w.shape, BF16),
-        in_specs=[whole, whole, whole, rows],
-        out_specs=rows,
-        scratch_shapes=[pltpu.VMEM((count, w.shape[1]), BF16)],
+        last_kernel,
+        name="finish",
+        grid=(steps,),
+        out_shape=(
+            jax.ShapeDtypeStruct(earlier.shape, BF16),
+            jax.ShapeDtypeStruct((toks, 2, width), BF16),
+        ),
+        in_specs=[
+            whole, whole, whole, rows,
+            pl.BlockSpec((2, toks // steps, width), lambda i: (0, i, 0)),
+        ],
+        out_specs=(rows, pl.BlockSpec((toks // steps, 2, width), lambda i: (i, 0, 0))),
+        scratch_shapes=[pltpu.VMEM((count, earlier.shape[1]), BF16)],
         compiler_params=pltpu.CompilerParams(vmem_limit_bytes=16 * 2**20),
         cost_estimate=pl.CostEstimate(
-            flops=4 * count * w.size, bytes_accessed=5_000_000, transcendentals=count * h.shape[1]
-        ),
-    )(x, h, w, earlier)
+            flops=2 * count * earlier.size, bytes_accessed=4_000_000, transcendentals=0
+        ),
+    )(x, h, ready_factors, earlier, pair)
 
 
 def body(routes, x_blocks, d_hidden, weights):
-    sections = lax.axis_size("section")
     experts = lax.axis_size("expert")
-    s = lax.axis_index("section")
     named = jnp.transpose(routes[0], (0, 2, 1))
     x = x_blocks.reshape(-1, x_blocks.shape[4])
     h = d_hidden.reshape(-1, d_hidden.shape[4])
     w = weights[0, 0]
     kept = x.shape[0] * 3 // 4
-    pair, most, x_last, h_last, w_held = exchange(named, x, h, w, named.shape[2] // experts, kept)
-    zero = jnp.zeros((), BF16)
-    d_in = jnp.stack(
-        [jnp.where(s == sections - 1, zero, pair[0]), jnp.where(s == 0, zero, pair[1])], axis=1
+    pair, most, x_last, h_last, ready_factors = exchange(
+        named, x, h, w, named.shape[2] // experts, kept
     )
-    d_weights = weight_sum(x_last, h_last, w_held, most)
+    d_weights, d_in = finish(x_last, h_last, ready_factors, most, pair)
     return (d_in[None], d_weights[None, None])
 
 

time: 64.1 us -> 62.4 us (0.973)
  the two profiles are of different devices: /device:TPU:1 before, /device:TPU:631 now
where the time goes in v3:
time: 62.4 us; the launch traced here: 62.2 us
  Pallas kernels  61.6 us (99%)
  between operations  0.64 us (1%)
    pallas_call x1, Pallas kernels, exchange(): pl.pallas_call(exchange_kernel, name='exchange', out_shape=(jax.ShapeDtyp...  59.1 us
    pallas_call x1, Pallas kernels, finish(): pl.pallas_call(last_kernel, name='finish', grid=(steps,), out_shape=(jax....  2.48 us

profile of v3, /device:TPU:631, one launch (start us, length us, event | category | flops | bytes accessed | tf_op | source)
XLA Modules:
  0.0 62.2 jit_solution(5399409332568869860)
XLA Ops:
  0.6 59.1 %exchange.1 = (bf16[2,64,1024]{2,1,0:T(8,128)(2,1)S(1)}, bf16[1024,768]{1,0:T(8,128)(2,1)S(1)}, bf16[96,1024]{1,0:T(8,128)(2,1)S(1)}, bf16[96,384]{1,0:T(8,128)(2,1)S(1)}, f32[3,96,384]{2,1,0:T(8,128)S(1)}) custom-call(s32[2,2,256]{2,1,0:T(2,128)} %bitcast.13, bf16[384,1024]{1,0:T(8,128)(2,1)} %bitcast.10, bf16[384,384]{1,0:T(8,128)(2,1)} %bitcast.11, ...), custom_call_target="tpu_custom_call" | custom-call | flops 3000000000 | bytes 8000000 | tf_op jit(solution)/shard_map/exchange/pallas_call | solution.py:230
  59.7 2.5 %finish.1 = (bf16[1024,768]{1,0:T(8,128)(2,1)}, bf16[64,2,1024]{2,1,0:T(2,128)(2,1)}) custom-call(bf16[96,1024]{1,0:T(8,128)(2,1)S(1)} %get-tuple-element.9.x, bf16[96,384]{1,0:T(8,128)(2,1)S(1)} %get-tuple-element.10.h, f32[3,96,384]{2,1,0:T(8,128)S(1)} %get-tuple-element.11.ready_factors, bf16[1024,768]{1,0:T(8,128)(2,1)S(1)} %get-tuple-element.12.earlier, ...), custom_call_target="tpu_custom_call" | custom-call | flops 150994944 | bytes 4000000 | tf_op jit(solution)/shard_map/finish/pallas_call | solution.py:297

commit v4 on v3

--- a/solution.py
+++ b/solution.py
@@ -25,8 +25,8 @@
 
 def exchange_kernel(
     routes, x_hbm, h_hbm, w_hbm,
-    d_out, most_out, x_last, h_last, last_factors,
-    x, h, w, g, part, far, near, mid, total, x_twin, h_twin, g_twin, acc,
+    d_out, most_out, x_turned, h_last, last_factors,
+    x, h, w, g, part, far, near, mid, total, x_twin, h_twin, acc,
     named_rows, in_sems, sends, recvs, ready,
 ):
     sections = lax.axis_size("section")
@@ -126,16 +126,13 @@
 
     kept = x_twin.shape[0]
     first = cap
-    kept, left = x_twin.shape[0], x_last.shape[0]
-    first = cap
-    head, middle, tail = pl.ds(0, first), pl.ds(first, kept - first), pl.ds(kept, left)
-    to_twin = [
-        send(8, x_hbm.at[head], x_twin.at[head], twin),
-        send(9, h.at[pl.ds(0, kept)], h_twin, twin),
-        send(10, x_hbm.at[middle], x_twin.at[middle], twin),
-        send(11, x_hbm.at[tail], x_last, twin),
-        send(12, h.at[tail], h_last, twin),
-    ]
+    count = x.shape[0] // 3
+    kept = h_twin.shape[1]
+    chunks = [pl.ds(i * count, count) for i in range(3)]
+    to_twin = [send(8, h.at[:, pl.ds(0, kept)], h_twin, twin)]
+    for i, rows in enumerate(chunks):
+        to_twin.append(send(9 + i, x_hbm.at[rows], x_twin.at[rows], twin))
+    to_twin.append(send(12, h.at[:, pl.ds(kept, ff - kept)], h_last, twin))
 
     loads[2].wait()
     loads[3].wait()
@@ -179,18 +176,22 @@
     mid[1] = (part[1, down_owner].astype(F32) + far[1].astype(F32)).astype(BF16)
     mid_down = send(5, mid.at[1], total.at[1], down)
 
-    def twin_chunk(start, count):
-        rows = pl.ds(start, count)
-        grad_gate, grad_up = gradients(h_twin[rows], *factors(x_twin[rows], w[...]))
-        g_twin[rows, :ff] = grad_gate
-        g_twin[rows, ff:] = grad_up
-        return lax.dot_general(
-            x_twin[rows], g_twin[rows], (((0,), (0,)), ((), ())), preferred_element_type=F32
+    def twin_chunk(rows):
+        up_pre, for_gate, for_up = factors(x_twin[rows], w[...])
+        for i, factor in enumerate((up_pre, for_gate, for_up)):
+            last_factors[i, rows] = factor[:, kept:]
+        grad_gate, grad_up = gradients(
+            h_twin[rows], up_pre[:, :kept], for_gate[:, :kept], for_up[:, :kept]
         )
+        turned = jnp.transpose(x_twin[rows])
+        x_turned[:, rows] = turned
+        acc[:, :kept] += jnp.dot(turned, grad_gate, preferred_element_type=F32)
+        acc[:, ff:ff + kept] += jnp.dot(turned, grad_up, preferred_element_type=F32)
 
     to_twin[0].wait_recv()
-    to_twin[1].wait_recv()
-    acc[...] += twin_chunk(0, first)
+    for i in range(2):
+        to_twin[1 + i].wait_recv()
+        twin_chunk(chunks[i])
 
     near_up.wait_recv()
     near_down.wait_recv()
@@ -205,12 +206,10 @@
     to_before = send(6, far.at[0], d_out.at[0], before)
     to_after = send(7, far.at[1], d_out.at[1], after)
 
-    to_twin[2].wait_recv()
-    most_out[...] = (acc[...] + twin_chunk(first, kept - first)).astype(BF16)
-
     to_twin[3].wait_recv()
-    for i, factor in enumerate(factors(x_last[...], w[...])):
-        last_factors[i] = factor
+    twin_chunk(chunks[2])
+    most_out[...] = acc[...].astype(BF16)
+
     for copy in (near_up, near_down, mid_up, mid_down):
         copy.wait_send()
     to_before.wait()
@@ -226,16 +225,16 @@
     anywhere = pl.BlockSpec(memory_space=pl.ANY)
     vmem = pl.BlockSpec(memory_space=pltpu.VMEM)
     block = (2, toks_owned, width)
-    left = x.shape[0] - kept
+    left = h.shape[1] - kept
     return pl.pallas_call(
         exchange_kernel,
         name="exchange",
         out_shape=(
             jax.ShapeDtypeStruct(block, BF16),
             jax.ShapeDtypeStruct(w.shape, BF16),
-            jax.ShapeDtypeStruct((left, width), BF16),
-            jax.ShapeDtypeStruct((left, h.shape[1]), BF16),
-            jax.ShapeDtypeStruct((3, left, h.shape[1]), F32),
+            jax.ShapeDtypeStruct((width, x.shape[0]), BF16),
+            jax.ShapeDtypeStruct((x.shape[0], left), BF16),
+            jax.ShapeDtypeStruct((3, x.shape[0], left), F32),
         ),
         in_specs=[hbm, hbm, hbm, hbm],
         out_specs=(anywhere, vmem, vmem, anywhere, vmem),
@@ -249,9 +248,8 @@
             pltpu.VMEM(block, BF16),
             pltpu.VMEM(block, BF16),
             pltpu.VMEM(block, BF16),
-            pltpu.VMEM((kept, width), BF16),
-            pltpu.VMEM((kept, h.shape[1]), BF16),
-            pltpu.VMEM((kept, w.shape[1]), BF16),
+            pltpu.VMEM(x.shape, BF16),
+            pltpu.VMEM((h.shape[0], kept), BF16),
             pltpu.VMEM(w.shape, F32),
             pltpu.VMEM(routes.shape, jnp.int32),
             pltpu.SemaphoreType.DMA((4,)),
@@ -268,51 +266,60 @@
     )(*(pltpu.with_memory_space_constraint(a, pltpu.HBM) for a in (routes, x, h, w)))
 
 
-def last_kernel(x, h, ready_factors, earlier, pair, d_weights, d_in, g):
-    tile = d_weights.shape[0]
-    step = pl.program_id(0)
-
-    @pl.when(step == 0)
-    def _():
-        ff = h.shape[1]
-        grad_gate, grad_up = gradients(h[...], *(ready_factors[i] for i in range(3)))
-        g[:, :ff] = grad_gate
-        g[:, ff:] = grad_up
-
-    columns = pl.ds(pl.multiple_of(step * tile, tile), tile)
-    product = lax.dot_general(
-        x[:, columns], g[...], (((0,), (0,)), ((), ())), preferred_element_type=F32
-    )
-    d_weights[...] = (earlier[...].astype(F32) + product).astype(BF16)
-    for r in range(2):
-        d_in[:, r, :] = pair[r]
-
-
-def finish(x, h, ready_factors, earlier, pair):
+def last_kernel(x_turned, h, ready_factors, earlier, pair, d_weights, d_in, product, woven, sems):
+    ff = earlier.shape[1] // 2
+    left = h.shape[1]
+    kept = ff - left
     steps = 4
+    tile = earlier.shape[0] // steps
+    copies = []
+
+    def put(src, dst):
+        copy = pltpu.make_async_copy(src, dst, sems.at[len(copies)])
+        copy.start()
+        copies.append(copy)
+
+    for start in (0, ff):
+        columns = pl.ds(start, kept)
+        put(earlier.at[:, columns], d_weights.at[:, columns])
+    g = gradients(h[...], *(ready_factors[i] for i in range(3)))
+    for i in range(steps):
+        rows = pl.ds(i * tile, tile)
+        for side in range(2):
+            columns = pl.ds(side * ff + kept, left)
+            more = jnp.dot(x_turned[rows], g[side], preferred_element_type=F32)
+            product[side, rows] = (earlier[rows, columns].astype(F32) + more).astype(BF16)
+            put(product.at[side, rows], d_weights.at[rows, columns])
+    for r in range(2):
+        woven[:, r, :] = pair[r]
+    put(woven, d_in)
+    for copy in copies:
+        copy.wait()
+
+
+def finish(x_turned, h, ready_factors, earlier, pair):
     toks, width = pair.shape[1:]
     whole = pl.BlockSpec(memory_space=pltpu.VMEM)
-    rows = pl.BlockSpec((earlier.shape[0] // steps, earlier.shape[1]), lambda i: (i, 0))
-    count = x.shape[0]
+    anywhere = pl.BlockSpec(memory_space=pl.ANY)
     return pl.pallas_call(
         last_kernel,
         name="finish",
-        grid=(steps,),
         out_shape=(
             jax.ShapeDtypeStruct(earlier.shape, BF16),
             jax.ShapeDtypeStruct((toks, 2, width), BF16),
         ),
-        in_specs=[
-            whole, whole, whole, rows,
-            pl.BlockSpec((2, toks // steps, width), lambda i: (0, i, 0)),
+        in_specs=[whole] * 5,
+        out_specs=(anywhere, anywhere),
+        scratch_shapes=[
+            pltpu.VMEM((2, earlier.shape[0], h.shape[1]), BF16),
+            pltpu.VMEM((toks, 2, width), BF16),
+            pltpu.SemaphoreType.DMA((11,)),
         ],
-        out_specs=(rows, pl.BlockSpec((toks // steps, 2, width), lambda i: (i, 0, 0))),
-        scratch_shapes=[pltpu.VMEM((count, earlier.shape[1]), BF16)],
         compiler_params=pltpu.CompilerParams(vmem_limit_bytes=16 * 2**20),
         cost_estimate=pl.CostEstimate(
-            flops=2 * count * earlier.size, bytes_accessed=4_000_000, transcendentals=0
-        ),
-    )(x, h, ready_factors, earlier, pair)
+            flops=600_000_000, bytes_accessed=4_000_000, transcendentals=0
+        ),
+    )(x_turned, h, ready_factors, earlier, pair)
 
 
 def body(routes, x_blocks, d_hidden, weights):
@@ -321,11 +328,11 @@
     x = x_blocks.reshape(-1, x_blocks.shape[4])
     h = d_hidden.reshape(-1, d_hidden.shape[4])
     w = weights[0, 0]
-    kept = x.shape[0] * 3 // 4
-    pair, most, x_last, h_last, ready_factors = exchange(
+    kept = h.shape[1] * 2 // 3
+    pair, most, x_turned, h_last, ready_factors = exchange(
         named, x, h, w, named.shape[2] // experts, kept
     )
-    d_weights, d_in = finish(x_last, h_last, ready_factors, most, pair)
+    d_weights, d_in = finish(x_turned, h_last, ready_factors, most, pair)
     return (d_in[None], d_weights[None, None])
 
 

time: 62.4 us -> 62.1 us (level)
  the two profiles are of different devices: /device:TPU:631 before, /device:TPU:240 now
where the time goes in v4:
time: 62.1 us; the launch traced here: 62 us
  Pallas kernels  61.3 us (99%)
  between operations  0.64 us (1%)
    pallas_call x1, Pallas kernels, exchange(): pl.pallas_call(exchange_kernel, name='exchange', out_shape=(jax.ShapeDtyp...  59.9 us
    pallas_call x1, Pallas kernels, finish(): pl.pallas_call(last_kernel, name='finish', out_shape=(jax.ShapeDtypeStruc...  1.43 us

profile of v4, /device:TPU:240, one launch (start us, length us, event | category | flops | bytes accessed | tf_op | source)
XLA Modules:
  0.0 62.0 jit_solution(16481050617092845001)
XLA Ops:
  0.6 59.9 %exchange.1 = (bf16[2,64,1024]{2,1,0:T(8,128)(2,1)S(1)}, bf16[1024,768]{1,0:T(8,128)(2,1)S(1)}, bf16[1024,384]{1,0:T(8,128)(2,1)S(1)}, bf16[384,128]{1,0:T(8,128)(2,1)S(1)}, f32[3,384,128]{2,1,0:T(8,128)S(1)}) custom-call(s32[2,2,256]{2,1,0:T(2,128)} %bitcast.13, bf16[384,1024]{1,0:T(8,128)(2,1)} %bitcast.10, bf16[384,384]{1,0:T(8,128)(2,1)} %bitcast.11, ...), custom_call_target="tpu_custom_call" | custom-call | flops 3000000000 | bytes 8000000 | tf_op jit(solution)/shard_map/exchange/pallas_call | solution.py:229
  60.5 1.4 %finish.1 = (bf16[1024,768]{1,0:T(8,128)(2,1)}, bf16[64,2,1024]{2,1,0:T(2,128)(2,1)}) custom-call(bf16[1024,384]{1,0:T(8,128)(2,1)S(1)} %get-tuple-element.9.x_turned, bf16[384,128]{1,0:T(8,128)(2,1)S(1)} %get-tuple-element.10.h, f32[3,384,128]{2,1,0:T(8,128)S(1)} %get-tuple-element.11.ready_factors, bf16[1024,768]{1,0:T(8,128)(2,1)S(1)} %get-tuple-element.12.earlier, ...), custom_call_target="tpu_custom_call" | custom-call | flops 600000000 | bytes 4000000 | tf_op jit(solution)/shard_map/finish/pallas_call | solution.py:304

commit v5 on v4

--- a/solution.py
+++ b/solution.py
@@ -188,11 +188,6 @@
         acc[:, :kept] += jnp.dot(turned, grad_gate, preferred_element_type=F32)
         acc[:, ff:ff + kept] += jnp.dot(turned, grad_up, preferred_element_type=F32)
 
-    to_twin[0].wait_recv()
-    for i in range(2):
-        to_twin[1 + i].wait_recv()
-        twin_chunk(chunks[i])
-
     near_up.wait_recv()
     near_down.wait_recv()
     mid_up.wait_recv()
@@ -206,8 +201,10 @@
     to_before = send(6, far.at[0], d_out.at[0], before)
     to_after = send(7, far.at[1], d_out.at[1], after)
 
-    to_twin[3].wait_recv()
-    twin_chunk(chunks[2])
+    to_twin[0].wait_recv()
+    for i in range(0, 3):
+        to_twin[1 + i].wait_recv()
+        twin_chunk(chunks[i])
     most_out[...] = acc[...].astype(BF16)
 
     for copy in (near_up, near_down, mid_up, mid_down):

time: 62.1 us -> 59.9 us (0.965)
  the two profiles are of different devices: /device:TPU:240 before, /device:TPU:55 now
where the time goes in v5:
time: 59.9 us; the launch traced here: 59.7 us
  Pallas kernels  59 us (98%)
  between operations  0.64 us (1%)
    pallas_call x1, Pallas kernels, exchange(): pl.pallas_call(exchange_kernel, name='exchange', out_shape=(jax.ShapeDtyp...  57.6 us
    pallas_call x1, Pallas kernels, finish(): pl.pallas_call(last_kernel, name='finish', out_shape=(jax.ShapeDtypeStruc...  1.43 us

profile of v5, /device:TPU:55, one launch (start us, length us, event | category | flops | bytes accessed | tf_op | source)
XLA Modules:
  0.0 59.7 jit_solution(3376867014172241045)
XLA Ops:
  0.6 57.6 %exchange.1 = (bf16[2,64,1024]{2,1,0:T(8,128)(2,1)S(1)}, bf16[1024,768]{1,0:T(8,128)(2,1)S(1)}, bf16[1024,384]{1,0:T(8,128)(2,1)S(1)}, bf16[384,128]{1,0:T(8,128)(2,1)S(1)}, f32[3,384,128]{2,1,0:T(8,128)S(1)}) custom-call(s32[2,2,256]{2,1,0:T(2,128)} %bitcast.13, bf16[384,1024]{1,0:T(8,128)(2,1)} %bitcast.10, bf16[384,384]{1,0:T(8,128)(2,1)} %bitcast.11, ...), custom_call_target="tpu_custom_call" | custom-call | flops 3000000000 | bytes 8000000 | tf_op jit(solution)/shard_map/exchange/pallas_call | solution.py:226
  58.2 1.4 %finish.1 = (bf16[1024,768]{1,0:T(8,128)(2,1)}, bf16[64,2,1024]{2,1,0:T(2,128)(2,1)}) custom-call(bf16[1024,384]{1,0:T(8,128)(2,1)S(1)} %get-tuple-element.9.x_turned, bf16[384,128]{1,0:T(8,128)(2,1)S(1)} %get-tuple-element.10.h, f32[3,384,128]{2,1,0:T(8,128)S(1)} %get-tuple-element.11.ready_factors, bf16[1024,768]{1,0:T(8,128)(2,1)S(1)} %get-tuple-element.12.earlier, ...), custom_call_target="tpu_custom_call" | custom-call | flops 600000000 | bytes 4000000 | tf_op jit(solution)/shard_map/finish/pallas_call | solution.py:301

commit v6 on v5

--- a/solution.py
+++ b/solution.py
@@ -169,12 +169,18 @@
         x[...], g[...], (((0,), (0,)), ((), ())), preferred_element_type=F32
     )
 
-    far_up.wait_recv()
-    mid[0] = (part[0, up_owner].astype(F32) + far[0].astype(F32)).astype(BF16)
-    mid_up = send(4, mid.at[0], total.at[0], up)
-    far_down.wait_recv()
-    mid[1] = (part[1, down_owner].astype(F32) + far[1].astype(F32)).astype(BF16)
-    mid_down = send(5, mid.at[1], total.at[1], down)
+    block = part.shape[2] // 2
+    halves = [pl.ds(i * block, block) for i in range(2)]
+    ways = ((far_up, up_owner, up), (far_down, down_owner, down))
+    mids = []
+    for arrived, owner, device in ways:
+        r = len(mids)
+        arrived.wait_recv()
+        mid[r] = (part[r, owner].astype(F32) + far[r].astype(F32)).astype(BF16)
+        mids.append([
+            send(13 + 2 * r + i, mid.at[r, rows], total.at[r, rows], device)
+            for i, rows in enumerate(halves)
+        ])
 
     def twin_chunk(rows):
         up_pre, for_gate, for_up = factors(x_twin[rows], w[...])
@@ -190,16 +196,21 @@
 
     near_up.wait_recv()
     near_down.wait_recv()
-    mid_up.wait_recv()
-    mid_down.wait_recv()
     far_up.wait_send()
     far_down.wait_send()
-    for r in range(2):
-        summed = part[r, e].astype(F32) + near[r].astype(F32) + total[r].astype(F32)
-        edge = s == (0 if r == 0 else sections - 1)
-        far[r] = jnp.where(edge, 0.0, summed).astype(BF16)
-    to_before = send(6, far.at[0], d_out.at[0], before)
-    to_after = send(7, far.at[1], d_out.at[1], after)
+    shifts = []
+    for i, rows in enumerate(halves):
+        for r, device in enumerate((before, after)):
+            mids[r][i].wait_recv()
+            summed = (
+                part[r, e, rows].astype(F32) + near[r, rows].astype(F32)
+                + total[r, rows].astype(F32)
+            )
+            edge = s == (0 if r == 0 else sections - 1)
+            far[r, rows] = jnp.where(edge, 0.0, summed).astype(BF16)
+            shifts.append(
+                send(4 + 2 * r + i, far.at[r, rows], d_out.at[r, rows], device)
+            )
 
     to_twin[0].wait_recv()
     for i in range(0, 3):
@@ -207,10 +218,10 @@
         twin_chunk(chunks[i])
     most_out[...] = acc[...].astype(BF16)
 
-    for copy in (near_up, near_down, mid_up, mid_down):
+    for copy in (near_up, near_down, *mids[0], *mids[1]):
         copy.wait_send()
-    to_before.wait()
-    to_after.wait()
+    for copy in shifts:
+        copy.wait()
     for copy in to_twin:
         copy.wait_send()
     to_twin[4].wait_recv()
@@ -250,8 +261,8 @@
             pltpu.VMEM(w.shape, F32),
             pltpu.VMEM(routes.shape, jnp.int32),
             pltpu.SemaphoreType.DMA((4,)),
-            pltpu.SemaphoreType.DMA((13,)),
-            pltpu.SemaphoreType.DMA((13,)),
+            pltpu.SemaphoreType.DMA((17,)),
+            pltpu.SemaphoreType.DMA((17,)),
             pltpu.SemaphoreType.REGULAR,
         ],
         compiler_params=pltpu.CompilerParams(

time: 59.9 us -> 59.9 us (level)
  the two profiles are of different devices: /device:TPU:55 before, /device:TPU:169 now
where the time goes in v6:
time: 59.9 us; the launch traced here: 59.7 us
  Pallas kernels  59 us (98%)
  between operations  0.64 us (1%)
    pallas_call x1, Pallas kernels, exchange(): pl.pallas_call(exchange_kernel, name='exchange', out_shape=(jax.ShapeDtyp...  57.6 us
    pallas_call x1, Pallas kernels, finish(): pl.pallas_call(last_kernel, name='finish', out_shape=(jax.ShapeDtypeStruc...  1.43 us

profile of v6, /device:TPU:169, one launch (start us, length us, event | category | flops | bytes accessed | tf_op | source)
XLA Modules:
  0.0 59.7 jit_solution(2860346329603816323)
XLA Ops:
  0.6 57.6 %exchange.1 = (bf16[2,64,1024]{2,1,0:T(8,128)(2,1)S(1)}, bf16[1024,768]{1,0:T(8,128)(2,1)S(1)}, bf16[1024,384]{1,0:T(8,128)(2,1)S(1)}, bf16[384,128]{1,0:T(8,128)(2,1)S(1)}, f32[3,384,128]{2,1,0:T(8,128)S(1)}) custom-call(s32[2,2,256]{2,1,0:T(2,128)} %bitcast.13, bf16[384,1024]{1,0:T(8,128)(2,1)} %bitcast.10, bf16[384,384]{1,0:T(8,128)(2,1)} %bitcast.11, ...), custom_call_target="tpu_custom_call" | custom-call | flops 3000000000 | bytes 8000000 | tf_op jit(solution)/shard_map/exchange/pallas_call | solution.py:237
  58.3 1.4 %finish.1 = (bf16[1024,768]{1,0:T(8,128)(2,1)}, bf16[64,2,1024]{2,1,0:T(2,128)(2,1)}) custom-call(bf16[1024,384]{1,0:T(8,128)(2,1)S(1)} %get-tuple-element.9.x_turned, bf16[384,128]{1,0:T(8,128)(2,1)S(1)} %get-tuple-element.10.h, f32[3,384,128]{2,1,0:T(8,128)S(1)} %get-tuple-element.11.ready_factors, bf16[1024,768]{1,0:T(8,128)(2,1)S(1)} %get-tuple-element.12.earlier, ...), custom_call_target="tpu_custom_call" | custom-call | flops 600000000 | bytes 4000000 | tf_op jit(solution)/shard_map/finish/pallas_call | solution.py:312
